TPU v7x, 32 devices: a whole 2x2x4 slice. The times are simulated.
32 devices in a mesh: replica: 8 (over y, x, core), shard: 4 (over z).
Axes of the slice: x: 2, y: 2, z: 4, core: 2. Of those that a mesh axis runs over, the one named last changes fastest.
Arguments:
- tokens: bfloat16 [8192, 1536], P(('replica', 'shard')), may hold values from -8 to 8
- cotangent: bfloat16 [8192, 1536], P(('replica', 'shard')), may hold values from -6 to 6
- attn_gain: bfloat16 [1536], P('shard'), may hold values from 0.5 to 1.5
- w_query: bfloat16 [1536, 1536], P('shard'), may hold values from -0.17860863 to 0.17860863
- w_key: bfloat16 [1536, 768], P('shard'), may hold values from -0.17860863 to 0.17860863
- w_value: bfloat16 [1536, 768], P('shard'), may hold values from -0.15625 to 0.15625
- w_out: bfloat16 [1536, 1536], P('shard'), may hold values from -0.625 to 0.625
- mlp_gain: bfloat16 [1536], P('shard'), may hold values from 0.5 to 1.5
- w_gate: bfloat16 [1536, 4096], P('shard'), may hold values from -0.15625 to 0.15625
- w_up: bfloat16 [1536, 4096], P('shard'), may hold values from -0.15625 to 0.15625
- w_down: bfloat16 [4096, 1536], P('shard'), may hold values from -0.09375 to 0.09375
Outputs:
- block_output: bfloat16 [8192, 1536], P(('replica', 'shard'))
- input_grad: float32 [8192, 1536], P(('replica', 'shard'))
- attn_gain_grad: float32 [1536], P('shard')
- query_grad: float32 [1536, 1536], P('shard')
- key_grad: float32 [1536, 768], P('shard')
- value_grad: float32 [1536, 768], P('shard')
- out_grad: float32 [1536, 1536], P('shard')
- mlp_gain_grad: float32 [1536], P('shard')
- gate_grad: float32 [1536, 4096], P('shard')
- up_grad: float32 [1536, 4096], P('shard')
- down_grad: float32 [4096, 1536], P('shard')
All inputs are finite; a program needn't handle non-finite values.
Results may differ from a plain program's by a relative error of at most 0.014.
Values may be sent and summed in bfloat16 or wider, within the bound.
No kernel may reach another device: no remote copies, remote signals or barrier semaphores. Data moves between devices by JAX's collectives and lax.ppermute only.
A program may use at most 384 MiB of HBM per device.

v0:
```python
import jax
import jax.numpy as jnp
from jax import lax
from jax.sharding import PartitionSpec as P

HEAD_DIM = 96
NORM_EPS = 1e-05
ROPE_BASE = 100000.0


def product(form, left, right):
    return jnp.einsum(form, left, right, preferred_element_type=jnp.float32)


def plain_dot(left, right):
    return jnp.dot(left, right, preferred_element_type=jnp.float32)


def outer_product(left, right):
    return lax.dot_general(
        left, right, (((0,), (0,)), ((), ())), preferred_element_type=jnp.float32
    )


def back_dot(left, right):
    return lax.dot_general(
        left, right, (((1,), (1,)), ((), ())), preferred_element_type=jnp.float32
    )


def rope_tables(length):
    half = HEAD_DIM // 2
    position = jnp.arange(length, dtype=jnp.float32)
    freqs = jnp.power(ROPE_BASE, -jnp.arange(half, dtype=jnp.float32) / half)
    angles = position[:, None] * freqs[None, :]
    return (jnp.cos(angles)[:, None, :], jnp.sin(angles)[:, None, :])


def rotate(values, cosine, sine):
    half = HEAD_DIM // 2
    first, second = (values[..., :half], values[..., half:])
    return jnp.concatenate([first * cosine - second * sine, second * cosine + first * sine], -1)


def unrotate(values, cosine, sine):
    half = HEAD_DIM // 2
    first, second = (values[..., :half], values[..., half:])
    return jnp.concatenate([first * cosine + second * sine, second * cosine - first * sine], -1)


def norm_forward(rows, norm_gain):
    inverse_rms = lax.rsqrt(jnp.mean(rows * rows, -1, keepdims=True) + NORM_EPS)
    return (rows * inverse_rms * norm_gain, inverse_rms)


def norm_backward(rows, inverse_rms, norm_gain, d_normed):
    scaled = d_normed * norm_gain
    d_rows = inverse_rms * scaled - rows * inverse_rms**3 * jnp.mean(
        scaled * rows, -1, keepdims=True
    )
    return (d_rows, jnp.sum(d_normed * rows * inverse_rms, 0))


def head_scores(query_block, key_head, block_start, key_pos):
    block_rows = query_block.shape[0]
    scores = product("qjd,kd->jqk", query_block, key_head) * HEAD_DIM ** (-0.5)
    query_pos = block_start + jnp.arange(block_rows, dtype=jnp.int32)
    causal = query_pos[:, None] >= key_pos[None, :]
    return jnp.where(causal, scores, -jnp.inf)


def head_forward(head_items):
    query_head, key_head, value_head = head_items
    length, groups = (query_head.shape[0], query_head.shape[1])
    block_rows = min(length, 512)
    blocks = length // block_rows
    query_blocks = query_head.reshape(blocks, block_rows, groups, HEAD_DIM)
    starts = jnp.arange(blocks, dtype=jnp.int32) * block_rows
    key_pos = jnp.arange(length, dtype=jnp.int32)

    def one_block(inputs):
        query_block, block_start = inputs
        scores = head_scores(query_block, key_head, block_start, key_pos)
        row_top = jnp.max(scores, -1, keepdims=True)
        log_total = row_top + jnp.log(jnp.sum(jnp.exp(scores - row_top), -1, keepdims=True))
        probs = jnp.exp(scores - log_total).astype(jnp.bfloat16)
        mixed = product("jqk,kd->qjd", probs, value_head).astype(jnp.bfloat16)
        return (mixed, log_total[..., 0])

    mixed, log_totals = lax.map(one_block, (query_blocks, starts))
    return (mixed.reshape(length, groups, HEAD_DIM), log_totals)


def attend(query_rot, key_rot, value_low):
    length, kv_heads = (key_rot.shape[0], key_rot.shape[1])
    groups = query_rot.shape[1] // kv_heads
    query_heads = jnp.moveaxis(query_rot.reshape(length, kv_heads, groups, HEAD_DIM), 1, 0)
    mixed, log_totals = lax.map(
        head_forward, (query_heads, jnp.moveaxis(key_rot, 1, 0), jnp.moveaxis(value_low, 1, 0))
    )
    return (jnp.moveaxis(mixed, 0, 1).reshape(length, kv_heads * groups * HEAD_DIM), log_totals)


def head_backward(head_items):
    query_head, key_head, value_head, d_head, log_totals = head_items
    length, groups = (query_head.shape[0], query_head.shape[1])
    block_rows = min(length, 512)
    blocks = length // block_rows
    query_blocks = query_head.reshape(blocks, block_rows, groups, HEAD_DIM)
    d_blocks = d_head.reshape(blocks, block_rows, groups, HEAD_DIM)
    starts = jnp.arange(blocks, dtype=jnp.int32) * block_rows
    key_pos = jnp.arange(length, dtype=jnp.int32)
    empty = jnp.zeros((length, HEAD_DIM), jnp.float32)

    def one_block(carry, inputs):
        query_block, d_block, log_total, block_start = inputs
        scores = head_scores(query_block, key_head, block_start, key_pos)
        probs = jnp.exp(scores - log_total[..., None])
        d_value = carry[1] + product("jqk,qjd->kd", probs.astype(jnp.bfloat16), d_block)
        d_probs = product("qjd,kd->jqk", d_block, value_head)
        delta = jnp.sum(probs * d_probs, -1, keepdims=True)
        d_scores = (probs * (d_probs - delta) * HEAD_DIM ** (-0.5)).astype(jnp.bfloat16)
        d_query = product("jqk,kd->qjd", d_scores, key_head)
        d_key = carry[0] + product("jqk,qjd->kd", d_scores, query_block)
        return ((d_key, d_value), d_query)

    (d_key, d_value), d_query = lax.scan(
        one_block, (empty, empty), (query_blocks, d_blocks, log_totals, starts)
    )
    return (d_query.reshape(length, groups, HEAD_DIM), d_key, d_value)


def attend_back(query_rot, key_rot, value_low, d_heads, log_totals):
    length, kv_heads = (key_rot.shape[0], key_rot.shape[1])
    groups = query_rot.shape[1] // kv_heads
    query_heads = jnp.moveaxis(query_rot.reshape(length, kv_heads, groups, HEAD_DIM), 1, 0)
    d_by_head = jnp.moveaxis(d_heads.reshape(length, kv_heads, groups, HEAD_DIM), 1, 0)
    d_query, d_key, d_value = lax.map(
        head_backward,
        (
            query_heads,
            jnp.moveaxis(key_rot, 1, 0),
            jnp.moveaxis(value_low, 1, 0),
            d_by_head,
            log_totals,
        ),
    )
    d_query = jnp.moveaxis(d_query, 0, 1).reshape(length, kv_heads * groups, HEAD_DIM)
    return (d_query, jnp.moveaxis(d_key, 0, 1), jnp.moveaxis(d_value, 0, 1))


def attention_forward(seq_in, norm_gain, w_query, w_key, w_value, w_out):
    length = seq_in.shape[0]
    kv_heads = w_key.shape[1] // HEAD_DIM
    rows = seq_in.astype(jnp.float32)
    normed, inverse_rms = norm_forward(rows, norm_gain.astype(jnp.float32))
    normed_low = normed.astype(jnp.bfloat16)
    query = plain_dot(normed_low, w_query).reshape(length, -1, HEAD_DIM)
    key = plain_dot(normed_low, w_key).reshape(length, kv_heads, HEAD_DIM)
    value_low = (
        plain_dot(normed_low, w_value).astype(jnp.bfloat16).reshape(length, kv_heads, HEAD_DIM)
    )
    cosine, sine = rope_tables(length)
    query_rot = rotate(query, cosine, sine).astype(jnp.bfloat16)
    key_rot = rotate(key, cosine, sine).astype(jnp.bfloat16)
    heads_low, log_totals = attend(query_rot, key_rot, value_low)
    middle = rows + plain_dot(heads_low, w_out)
    return (middle, (inverse_rms, normed_low, query_rot, key_rot, value_low, heads_low, log_totals))


def mlp_forward(middle, norm_gain, w_gate, w_up, w_down):
    normed, inverse_rms = norm_forward(middle, norm_gain.astype(jnp.float32))
    normed_low = normed.astype(jnp.bfloat16)
    gate = plain_dot(normed_low, w_gate)
    upward = plain_dot(normed_low, w_up)
    active = (jax.nn.silu(gate) * upward).astype(jnp.bfloat16)
    output = (middle + plain_dot(active, w_down)).astype(jnp.bfloat16)
    return (output, (inverse_rms, normed_low, gate, upward, active))


def mlp_backward(middle, seq_cot, norm_gain, w_gate, w_up, w_down, saved):
    inverse_rms, normed_low, gate, upward, active = saved
    cot_rows = seq_cot.astype(jnp.float32)
    d_active = back_dot(seq_cot, w_down)
    sigmoid_gate = jax.nn.sigmoid(gate)
    d_gate = (d_active * upward * sigmoid_gate * (1.0 + gate * (1.0 - sigmoid_gate))).astype(
        jnp.bfloat16
    )
    d_upward = (d_active * gate * sigmoid_gate).astype(jnp.bfloat16)
    d_normed = back_dot(d_gate, w_gate) + back_dot(d_upward, w_up)
    d_rows, d_gain = norm_backward(middle, inverse_rms, norm_gain.astype(jnp.float32), d_normed)
    return (cot_rows + d_rows, d_gain, (normed_low, d_gate, d_upward, active, seq_cot))


def mlp_owned(gathered, part_index, width_rows, hidden_rows):
    normed_all, d_gate_all, d_upward_all, active_all, cot_all = gathered
    own_normed = lax.dynamic_slice_in_dim(normed_all, part_index * width_rows, width_rows, 1)
    own_active = lax.dynamic_slice_in_dim(active_all, part_index * hidden_rows, hidden_rows, 1)
    return (
        outer_product(own_normed, d_gate_all),
        outer_product(own_normed, d_upward_all),
        outer_product(own_active, cot_all),
    )


def attention_backward(seq_in, d_middle, norm_gain, w_query, w_key, w_value, w_out, saved):
    inverse_rms, normed_low, query_rot, key_rot, value_low, heads_low, log_totals = saved
    length = seq_in.shape[0]
    rows = seq_in.astype(jnp.float32)
    d_middle_low = d_middle.astype(jnp.bfloat16)
    d_heads = back_dot(d_middle_low, w_out).astype(jnp.bfloat16)
    d_query, d_key, d_value = attend_back(query_rot, key_rot, value_low, d_heads, log_totals)
    cosine, sine = rope_tables(length)
    d_query_low = unrotate(d_query, cosine, sine).astype(jnp.bfloat16).reshape(length, -1)
    d_key_low = unrotate(d_key, cosine, sine).astype(jnp.bfloat16).reshape(length, -1)
    d_value_low = d_value.astype(jnp.bfloat16).reshape(length, -1)
    d_normed = (
        back_dot(d_query_low, w_query) + back_dot(d_key_low, w_key) + back_dot(d_value_low, w_value)
    )
    d_rows, d_gain = norm_backward(rows, inverse_rms, norm_gain.astype(jnp.float32), d_normed)
    factors = (normed_low, d_query_low, d_key_low, d_value_low, heads_low, d_middle_low)
    return (d_middle + d_rows, d_gain, factors)


def attn_owned(gathered, part_index, width_rows):
    normed_all, d_query_all, d_key_all, d_value_all, heads_all, d_middle_all = gathered
    own_normed = lax.dynamic_slice_in_dim(normed_all, part_index * width_rows, width_rows, 1)
    own_heads = lax.dynamic_slice_in_dim(heads_all, part_index * width_rows, width_rows, 1)
    return (
        outer_product(own_normed, d_query_all),
        outer_product(own_normed, d_key_all),
        outer_product(own_normed, d_value_all),
        outer_product(own_heads, d_middle_all),
    )


def on_device(
    tokens, cotangent, attn_gain, w_query, w_key, w_value, w_out, mlp_gain, w_gate, w_up, w_down
):
    part_index = lax.axis_index("shard")
    attn_full = (
        lax.all_gather(attn_gain, "shard", axis=0, tiled=True),
        lax.all_gather(w_query, "shard", axis=0, tiled=True),
        lax.all_gather(w_key, "shard", axis=0, tiled=True),
        lax.all_gather(w_value, "shard", axis=0, tiled=True),
        lax.all_gather(w_out, "shard", axis=0, tiled=True),
    )
    middle, attn_saved = attention_forward(
        tokens, attn_full[0], attn_full[1], attn_full[2], attn_full[3], attn_full[4]
    )
    mlp_full = (
        lax.all_gather(mlp_gain, "shard", axis=0, tiled=True),
        lax.all_gather(w_gate, "shard", axis=0, tiled=True),
        lax.all_gather(w_up, "shard", axis=0, tiled=True),
        lax.all_gather(w_down, "shard", axis=0, tiled=True),
    )
    block_output, mlp_saved = mlp_forward(
        middle, mlp_full[0], mlp_full[1], mlp_full[2], mlp_full[3]
    )
    mlp_back = (
        lax.all_gather(mlp_gain, "shard", axis=0, tiled=True),
        lax.all_gather(w_gate, "shard", axis=0, tiled=True),
        lax.all_gather(w_up, "shard", axis=0, tiled=True),
        lax.all_gather(w_down, "shard", axis=0, tiled=True),
    )
    d_middle, mlp_gain_term, mlp_factors = mlp_backward(
        middle, cotangent, mlp_back[0], mlp_back[1], mlp_back[2], mlp_back[3], mlp_saved
    )
    gathered = (
        lax.all_gather(mlp_factors[0], "shard", axis=0, tiled=True),
        lax.all_gather(mlp_factors[1], "shard", axis=0, tiled=True),
        lax.all_gather(mlp_factors[2], "shard", axis=0, tiled=True),
        lax.all_gather(mlp_factors[3], "shard", axis=0, tiled=True),
        lax.all_gather(mlp_factors[4], "shard", axis=0, tiled=True),
    )
    owned_rows = mlp_owned(gathered, part_index, w_gate.shape[0], w_down.shape[0])
    mlp_sums = lax.psum((owned_rows[0], owned_rows[1], owned_rows[2]), "replica")
    attn_back = (
        lax.all_gather(attn_gain, "shard", axis=0, tiled=True),
        lax.all_gather(w_query, "shard", axis=0, tiled=True),
        lax.all_gather(w_key, "shard", axis=0, tiled=True),
        lax.all_gather(w_value, "shard", axis=0, tiled=True),
        lax.all_gather(w_out, "shard", axis=0, tiled=True),
    )
    input_grad, attn_gain_term, attn_factors = attention_backward(
        tokens,
        d_middle,
        attn_back[0],
        attn_back[1],
        attn_back[2],
        attn_back[3],
        attn_back[4],
        attn_saved,
    )
    gathered = (
        lax.all_gather(attn_factors[0], "shard", axis=0, tiled=True),
        lax.all_gather(attn_factors[1], "shard", axis=0, tiled=True),
        lax.all_gather(attn_factors[2], "shard", axis=0, tiled=True),
        lax.all_gather(attn_factors[3], "shard", axis=0, tiled=True),
        lax.all_gather(attn_factors[4], "shard", axis=0, tiled=True),
        lax.all_gather(attn_factors[5], "shard", axis=0, tiled=True),
    )
    owned_rows = attn_owned(gathered, part_index, w_query.shape[0])
    gains = (
        lax.psum_scatter(attn_gain_term, "shard", scatter_dimension=0, tiled=True),
        lax.psum_scatter(mlp_gain_term, "shard", scatter_dimension=0, tiled=True),
    )
    attn_sums = lax.psum(
        (gains[0], owned_rows[0], owned_rows[1], owned_rows[2], owned_rows[3], gains[1]), "replica"
    )
    attn_done = (attn_sums[0], attn_sums[1], attn_sums[2], attn_sums[3], attn_sums[4])
    mlp_done = (attn_sums[5], mlp_sums[0], mlp_sums[1], mlp_sums[2])
    return (
        block_output,
        input_grad,
        attn_done[0],
        attn_done[1],
        attn_done[2],
        attn_done[3],
        attn_done[4],
        mlp_done[0],
        mlp_done[1],
        mlp_done[2],
        mlp_done[3],
    )


def solution(mesh):
    return jax.shard_map(
        on_device,
        mesh=mesh,
        in_specs=(
            P(("replica", "shard"), None),
            P(("replica", "shard"), None),
            P("shard"),
            P("shard", None),
            P("shard", None),
            P("shard", None),
            P("shard", None),
            P("shard"),
            P("shard", None),
            P("shard", None),
            P("shard", None),
        ),
        out_specs=(
            P(("replica", "shard"), None),
            P(("replica", "shard"), None),
            P("shard"),
            P("shard", None),
            P("shard", None),
            P("shard", None),
            P("shard", None),
            P("shard"),
            P("shard", None),
            P("shard", None),
            P("shard", None),
        ),
        check_vma=False,
    )
```

profile of v0, /device:TPU:0, one launch (start us, length us, event | category | flops | bytes accessed | tf_op | source)
XLA Modules:
  0.0 2237.3 jit_solution(7603063944708746006)
XLA Ops:
  12.0 13.7 all-gather
  27.6 12.5 all-gather.1
  40.1 22.4 all-gather.21.cloned.1.call-done
  62.4 2.7 convolution_convert_fusion.2
  66.1 46.7 %all-gather.23.cloned.1.call-done = bf16[1536,768]{1,0:T(8,128)(2,1)} async-done(((bf16[384,768]{1,0:T(8,128)(2,1)}), bf16[1536,768]{1,0:T(8,128)(2,1)}) %all-gather.23.cloned.1.call-update) | async-done | bytes 2359312 | tf_op jit(solution)/shard_map/all_gather | solution.py:244
  112.8 2.7 fusion.91
  116.4 86.1 %all-gather.25.cloned.1.call-done = bf16[1536,1536]{1,0:T(8,128)(2,1)} async-done(((bf16[384,1536]{1,0:T(8,128)(2,1)}), bf16[1536,1536]{1,0:T(8,128)(2,1)}) %all-gather.25.cloned.1.call-update) | async-done | bytes 4718608 | tf_op jit(solution)/shard_map/all_gather | solution.py:243
  202.5 4.3 fusion.92
  207.1 18.5 while.10
  225.6 66.1 %all-gather.27.cloned.1.call-done = bf16[1536,1536]{1,0:T(8,128)(2,1)} async-done(((bf16[384,1536]{1,0:T(8,128)(2,1)}), bf16[1536,1536]{1,0:T(8,128)(2,1)}) %all-gather.27.cloned.1.call-update) | async-done | bytes 4718608 | tf_op jit(solution)/shard_map/all_gather | solution.py:246
  291.8 3.8 multiply_reduce_fusion.3
  295.8 214.0 %all-gather.29.cloned.1.call-done = bf16[1536,4096]{1,0:T(8,128)(2,1)} async-done(((bf16[384,4096]{1,0:T(8,128)(2,1)}), bf16[1536,4096]{1,0:T(8,128)(2,1)}) %all-gather.29.cloned.1.call-update) | async-done | bytes 12582928 | tf_op jit(solution)/shard_map/all_gather | solution.py:253
  509.8 9.5 fusion.93
  519.3 208.3 %all-gather.31.cloned.1.call-done = bf16[1536,4096]{1,0:T(8,128)(2,1)} async-done(((bf16[384,4096]{1,0:T(8,128)(2,1)}), bf16[1536,4096]{1,0:T(8,128)(2,1)}) %all-gather.31.cloned.1.call-update) | async-done | bytes 12582928 | tf_op jit(solution)/shard_map/all_gather | solution.py:254
  727.7 10.4 fusion.94
  738.1 207.5 %all-gather.33.cloned.1.call-done = bf16[4096,1536]{1,0:T(8,128)(2,1)} async-done(((bf16[1024,1536]{1,0:T(8,128)(2,1)}), bf16[4096,1536]{1,0:T(8,128)(2,1)}) %all-gather.33.cloned.1.call-update) | async-done | bytes 12582928 | tf_op jit(solution)/shard_map/all_gather | solution.py:255
  945.6 11.7 multiply_convert_fusion
  957.3 9.8 fusion.95
  967.1 9.4 multiply_reduce_fusion.1
  976.6 1.9 fusion.89
  978.5 4.0 convolution_convert_fusion.1
  983.7 61.8 %while.27 = (s32[]{:T(128)}, f32[8,256,2,96]{1,3,2,0:T(8,128)}, f32[8,256,96]{1,2,0:T(8,128)}, bf16[8,256,96]{1,2,0:T(8,128)(2,1)}, bf16[8,256,96]{1,2,0:T(8,128...) while((s32[]{:T(128)}, f32[8,256,2,96]{1,3,2,0:T(8,128)}, ...), condition=%wide.region_9.10_spmd, body=%wide.region_7.9_spmd.sunk | while | flops 127731200 | bytes 6843505 | solution.py:138
  986.1 1.8 fusion.165
  987.9 1.8 fusion.166
  993.8 1.8 fusion.165
  995.6 1.8 fusion.166
  1001.5 1.8 fusion.165
  1003.3 1.8 fusion.166
  1011.0 1.8 fusion.166
  1018.8 1.8 fusion.166
  1024.7 1.8 fusion.165
  1026.5 1.8 fusion.166
  1034.2 1.8 fusion.166
  1041.9 1.8 fusion.166
  1055.3 28.3 %all-gather.39.cloned.1.call-done = bf16[1024,768]{0,1:T(8,128)(2,1)} async-done(((bf16[256,768]{0,1:T(8,128)(2,1)}), bf16[1024,768]{0,1:T(8,128)(2,1)}) %all-gather.39.cloned.1.call-update) | async-done | bytes 1572880 | tf_op jit(solution)/shard_map/all_gather | solution.py:298
  1083.6 3.5 fusion.76
  1087.1 33.9 %all-gather.41.cloned.1.call-done = bf16[1024,768]{0,1:T(8,128)(2,1)} async-done(((bf16[256,768]{0,1:T(8,128)(2,1)}), bf16[1024,768]{0,1:T(8,128)(2,1)}) %all-gather.41.cloned.1.call-update) | async-done | bytes 1572880 | tf_op jit(solution)/shard_map/all_gather | solution.py:299
  1120.9 3.5 fusion.74
  1124.4 59.7 %all-gather.37.cloned.1.call-done = bf16[1024,1536]{0,1:T(8,128)(2,1)} async-done(((bf16[256,1536]{0,1:T(8,128)(2,1)}), bf16[1024,1536]{0,1:T(8,128)(2,1)}) %all-gather.37.cloned.1.call-update) | async-done | bytes 3145744 | tf_op jit(solution)/shard_map/all_gather | solution.py:297
  1184.1 5.0 fusion.78
  1189.1 58.0 %all-gather.43.cloned.1.call-done = bf16[1024,1536]{0,1:T(8,128)(2,1)} async-done(((bf16[256,1536]{0,1:T(8,128)(2,1)}), bf16[1024,1536]{0,1:T(8,128)(2,1)}) %all-gather.43.cloned.1.call-update) | async-done | bytes 3145744 | tf_op jit(solution)/shard_map/all_gather | solution.py:300
  1247.2 63.8 %all-gather.45.cloned.1.call-done = bf16[1024,1536]{1,0:T(8,128)(2,1)} async-done(((bf16[256,1536]{1,0:T(8,128)(2,1)}), bf16[1024,1536]{1,0:T(8,128)(2,1)}) %all-gather.45.cloned.1.call-update) | async-done | bytes 3145744 | tf_op jit(solution)/shard_map/all_gather | solution.py:301
  1311.0 4.9 fusion.68
  1315.9 58.6 %all-gather.47.cloned.1.call-done = bf16[1024,1536]{1,0:T(8,128)(2,1)} async-done(((bf16[256,1536]{1,0:T(8,128)(2,1)}), bf16[1024,1536]{1,0:T(8,128)(2,1)}) %all-gather.47.cloned.1.call-update) | async-done | bytes 3145744 | tf_op jit(solution)/shard_map/all_gather | solution.py:270
  1374.5 149.7 %all-gather.49.cloned.1.call-done = bf16[1024,4096]{1,0:T(8,128)(2,1)} async-done(((bf16[256,4096]{1,0:T(8,128)(2,1)}), bf16[1024,4096]{1,0:T(8,128)(2,1)}) %all-gather.49.cloned.1.call-update) | async-done | bytes 8388624 | tf_op jit(solution)/shard_map/all_gather | solution.py:271
  1524.2 10.1 fusion.72
  1534.4 139.7 %all-gather.51.cloned.1.call-done = bf16[1024,4096]{1,0:T(8,128)(2,1)} async-done(((bf16[256,4096]{1,0:T(8,128)(2,1)}), bf16[1024,4096]{1,0:T(8,128)(2,1)}) %all-gather.51.cloned.1.call-update) | async-done | bytes 8388624 | tf_op jit(solution)/shard_map/all_gather | solution.py:272
  1674.0 9.8 fusion.70
  1683.9 53.2 %all-gather.55.cloned.1.call-done = bf16[1024,1536]{1,0:T(8,128)(2,1)} async-done(((bf16[256,1536]{1,0:T(8,128)(2,1)}), bf16[1024,1536]{1,0:T(8,128)(2,1)}) %all-gather.55.cloned.1.call-update) | async-done | bytes 3145744 | tf_op jit(solution)/shard_map/all_gather | solution.py:274
  1737.1 149.7 %all-gather.53.cloned.1.call-done = bf16[1024,4096]{1,0:T(8,128)(2,1)} async-done(((bf16[256,4096]{1,0:T(8,128)(2,1)}), bf16[1024,4096]{1,0:T(8,128)(2,1)}) %all-gather.53.cloned.1.call-update) | async-done | bytes 8388624 | tf_op jit(solution)/shard_map/all_gather | solution.py:273
  1886.8 8.9 fusion.57
  1897.7 4.5 fusion.96
  1903.9 2.3 fusion.67
  1906.2 15.5 all-reduce.4
  1921.9 13.3 all-reduce.2
  1935.2 3.7 fusion.64
  1938.9 7.7 fusion.56
  1946.5 263.5 %all-reduce.7.cloned.1.call-done = (f32[384,1536]{1,0:T(8,128)}, f32[384,768]{1,0:T(8,128)}, f32[384,768]{1,0:T(8,128)}, f32[384,1536]{1,0:T(8,128)}, f32[384,40...) async-done(((f32[384,1536]{1,0:T(8,128)}, f32[384,768]{1,0:T(8,128)}, f32[384,768]{1,0:T(8,128)}, f32[384,1536]{1,0:T(8,128)}, f32[384,4096]{1,0:T(8,128)}, ...) | async-done | bytes 25952272 | tf_op jit(solution)/shard_map/psum | solution.py:308
  2210.0 3.4 copy.91
  2213.4 2.5 copy.92
  2215.9 2.4 copy.93
  2219.7 3.2 copy.95
  2224.4 2.9 copy.96
  2227.9 2.7 copy.97
  (205 shorter events, 84.2 us)
Async XLA Ops:
  7.2 55.3 %all-gather.21.cloned.1.call-start = ((), (), s32[]{:S(2)}) async-start(), calls=%async_computation | async-start | bytes 2949120 | tf_op jit(solution)/shard_map/all_gather | solution.py:245
  7.9 104.9 %all-gather.23.cloned.1.call-start = ((), (), s32[]{:S(2)}) async-start(), calls=%async_computation.1 | async-start | bytes 2949120 | tf_op jit(solution)/shard_map/all_gather | solution.py:244
  8.7 193.9 %all-gather.25.cloned.1.call-start = ((), (), s32[]{:S(2)}) async-start(), calls=%async_computation.2 | async-start | bytes 5898240 | tf_op jit(solution)/shard_map/all_gather | solution.py:243
  9.4 282.4 %all-gather.27.cloned.1.call-start = ((), (), s32[]{:S(2)}) async-start(), calls=%async_computation.3 | async-start | bytes 5898240 | tf_op jit(solution)/shard_map/all_gather | solution.py:246
  10.0 499.9 %all-gather.29.cloned.1.call-start = ((), (), s32[]{:S(2)}) async-start(), calls=%async_computation.4 | async-start | bytes 15728640 | tf_op jit(solution)/shard_map/all_gather | solution.py:253
  10.6 1.4 copy-start.13
  10.6 717.1 %all-gather.31.cloned.1.call-start = ((), (), s32[]{:S(2)}) async-start(), calls=%async_computation.5 | async-start | bytes 15728640 | tf_op jit(solution)/shard_map/all_gather | solution.py:254
  11.1 14.6 copy-start
  11.2 934.5 %all-gather.33.cloned.1.call-start = ((), (), s32[]{:S(2)}) async-start(), calls=%async_computation.6 | async-start | bytes 15728640 | tf_op jit(solution)/shard_map/all_gather | solution.py:255
  11.9 15.6 copy-start.14
  11.9 1043.4 %all-gather.35.cloned.1.call-start = ((), (), s32[]{:S(2)}) async-start(), calls=%async_computation.7 | async-start | bytes 3932160 | tf_op jit(solution)/shard_map/all_gather | solution.py:296
  27.2 1056.4 %all-gather.39.cloned.1.call-start = ((), (), s32[]{:S(2)}) async-start(), calls=%async_computation.9 | async-start | bytes 1966080 | tf_op jit(solution)/shard_map/all_gather | solution.py:298
  40.1 72.7 %copy-start.5 = (bf16[256,1536]{1,0:T(8,128)(2,1)S(1)}, bf16[256,1536]{1,0:T(8,128)(2,1)}, u32[]{:S(2)}) copy-start(bf16[256,1536]{1,0:T(8,128)(2,1)} %fusion.61) | copy-start | bytes 2359300
  225.6 66.2 %copy-start.11 = (bf16[8,256,2,96]{1,3,2,0:T(8,128)(2,1)}, bf16[8,256,2,96]{1,3,2,0:T(8,128)(2,1)S(1)}, u32[]{:S(2)}) copy-start(bf16[8,256,2,96]{1,3,2,0:T(8,128)(2,1)S(1)} %get-tuple-element.458) | copy-start | bytes 2359300
  225.6 70.0 %copy-start.1 = (bf16[8,256,2,96]{1,3,2,0:T(8,128)(2,1)}, bf16[8,256,2,96]{1,3,2,0:T(8,128)(2,1)S(1)}, u32[]{:S(2)}) copy-start(bf16[8,256,2,96]{1,3,2,0:T(8,128)(2,1)S(1)} %get-tuple-element.144) | copy-start | bytes 2359300
  295.8 214.0 %copy-start.6 = (bf16[256,1536]{1,0:T(8,128)(2,1)}, bf16[256,1536]{1,0:T(8,128)(2,1)S(1)}, u32[]{:S(2)}) copy-start(bf16[256,1536]{1,0:T(8,128)(2,1)S(1)} %multiply_convert_fusion.3) | copy-start | bytes 2359300
  519.3 426.3 %copy-start.3 = (bf16[256,1536]{1,0:T(8,128)(2,1)S(1)}, bf16[256,1536]{1,0:T(8,128)(2,1)}, u32[]{:S(2)}) copy-start(bf16[256,1536]{1,0:T(8,128)(2,1)} %param.16) | copy-start | bytes 2359300
  1047.5 73.4 %all-gather.41.cloned.1.call-start = ((), (), s32[]{:S(2)}) async-start(), calls=%async_computation.10 | async-start | bytes 1966080 | tf_op jit(solution)/shard_map/all_gather | solution.py:299
  1048.1 136.1 %all-gather.37.cloned.1.call-start = ((), (), s32[]{:S(2)}) async-start(), calls=%async_computation.8 | async-start | bytes 3932160 | tf_op jit(solution)/shard_map/all_gather | solution.py:297
  1050.8 196.4 %all-gather.43.cloned.1.call-start = ((), (), s32[]{:S(2)}) async-start(), calls=%async_computation.11 | async-start | bytes 3932160 | tf_op jit(solution)/shard_map/all_gather | solution.py:300
  1051.4 259.6 %all-gather.45.cloned.1.call-start = ((), (), s32[]{:S(2)}) async-start(), calls=%async_computation.12 | async-start | bytes 3932160 | tf_op jit(solution)/shard_map/all_gather | solution.py:301
  1052.1 322.4 %all-gather.47.cloned.1.call-start = ((), (), s32[]{:S(2)}) async-start(), calls=%async_computation.13 | async-start | bytes 3932160 | tf_op jit(solution)/shard_map/all_gather | solution.py:270
  1052.7 471.5 %all-gather.49.cloned.1.call-start = ((), (), s32[]{:S(2)}) async-start(), calls=%async_computation.14 | async-start | bytes 10485760 | tf_op jit(solution)/shard_map/all_gather | solution.py:271
  1053.3 620.8 %all-gather.51.cloned.1.call-start = ((), (), s32[]{:S(2)}) async-start(), calls=%async_computation.15 | async-start | bytes 10485760 | tf_op jit(solution)/shard_map/all_gather | solution.py:272
  1053.9 683.3 %all-gather.55.cloned.1.call-start = ((), (), s32[]{:S(2)}) async-start(), calls=%async_computation.17 | async-start | bytes 3932160 | tf_op jit(solution)/shard_map/all_gather | solution.py:274
  1054.5 832.4 %all-gather.53.cloned.1.call-start = ((), (), s32[]{:S(2)}) async-start(), calls=%async_computation.16 | async-start | bytes 10485760 | tf_op jit(solution)/shard_map/all_gather | solution.py:273
  1055.0 1155.0 %all-reduce.7.cloned.1.call-start = ((), (), s32[]{:S(2)}) async-start(), calls=%async_computation.18 | async-start | bytes 51904512 | tf_op jit(solution)/shard_map/psum | solution.py:308
  1895.8 0.7 copy-start.15
  1895.8 1.9 copy-start.4
  1897.7 4.5 copy-start.2
  1897.7 4.5 copy-start.9
  1902.2 1.7 copy-start.7
  1902.2 1.7 copy-start.12
  1935.2 3.7 copy-start.10
  2210.0 9.7 slice-start.4
  2213.4 4.9 copy-start.8
  2213.4 6.3 slice-start.5
  2218.3 4.7 slice-start.2
  2219.7 4.7 slice-start.3
  2219.7 7.6 slice-start
  2224.4 3.5 slice-start.1
Sparse Core Ops, SparseCore 0:
  9.6 52.8 all-gather.20
  64.0 48.7 all-gather.22
  114.3 88.1 all-gather.24
  203.9 87.7 all-gather.26
  293.2 216.5 all-gather.28
  511.2 216.3 all-gather.30
  729.2 216.3 all-gather.32
  947.8 61.6 all-gather.34
  1047.6 35.8 all-gather.38
  1085.0 35.9 all-gather.40
  1122.5 61.6 all-gather.36
  1185.6 61.5 all-gather.42
  1249.3 61.6 all-gather.44
  1312.4 62.0 all-gather.46
  1375.9 148.2 all-gather.48
  1526.2 147.7 all-gather.50
  1675.5 61.6 all-gather.54
  1738.5 148.2 all-gather.52
  1895.9 314.0 all-reduce.6
where the time goes:
time: 2240 us
  waiting for transfers between devices  1920 us (86%)
  matrix products  208 us (9%)
  blocking collectives  55 us (2%)
  local copies, waits for them, and re-layouts  24.9 us (1%)
    psum x1, waiting for transfers between devices, on_device(): lax.psum((gains[0], owned_rows[0], owned_rows[1], owned_rows[2], owned_ro...  263 us
    all_gather x1, waiting for transfers between devices, on_device(): lax.all_gather(w_gate, 'shard', axis=0, tiled=True)  214 us
    all_gather x1, waiting for transfers between devices, on_device(): lax.all_gather(w_up, 'shard', axis=0, tiled=True)  208 us
    all_gather x1, waiting for transfers between devices, on_device(): lax.all_gather(w_down, 'shard', axis=0, tiled=True)  208 us
    all_gather x1, waiting for transfers between devices, on_device(): lax.all_gather(mlp_factors[3], 'shard', axis=0, tiled=True)  150 us
    all_gather x1, waiting for transfers between devices, on_device(): lax.all_gather(mlp_factors[1], 'shard', axis=0, tiled=True)  150 us
    all_gather x1, waiting for transfers between devices, on_device(): lax.all_gather(mlp_factors[2], 'shard', axis=0, tiled=True)  140 us
    all_gather x1, waiting for transfers between devices, on_device(): lax.all_gather(w_query, 'shard', axis=0, tiled=True)  86.1 us
  transfers between devices with their start and end apart: 19, of which 18 were waited for; matrix products, arithmetic and copies ran while one was open for 10% of the time, Pallas kernels for 0%

commit v1 on v0

--- a/solution.py
+++ b/solution.py
@@ -6,6 +6,17 @@
 HEAD_DIM = 96
 NORM_EPS = 1e-05
 ROPE_BASE = 100000.0
+
+
+def collect(x, axis, dim):
+    ways = lax.axis_size(axis)
+    pieces = [x]
+    for far in range(1, ways):
+        pieces.append(
+            lax.ppermute(pieces[far - 1], axis, [(d, (d - 1) % ways) for d in range(ways)])
+        )
+    line = jnp.concatenate(pieces, axis=dim)
+    return jnp.roll(line, lax.axis_index(axis) * x.shape[dim], axis=dim)
 
 
 def product(form, left, right):
@@ -251,7 +262,7 @@
     mlp_full = (
         lax.all_gather(mlp_gain, "shard", axis=0, tiled=True),
         lax.all_gather(w_gate, "shard", axis=0, tiled=True),
-        lax.all_gather(w_up, "shard", axis=0, tiled=True),
+        collect(w_up, "shard", 0),
         lax.all_gather(w_down, "shard", axis=0, tiled=True),
     )
     block_output, mlp_saved = mlp_forward(

time: 2240 us -> 2410 us (1.076)
  blocking collectives: 55 us -> 249 us
  waiting for transfers between devices: 1920 us -> 1840 us
  local copies, waits for them, and re-layouts: 24.9 us -> 60.2 us
    all_gather x1, blocking collectives: 13.7 us -> 113 us  [on_device(): lax.all_gather(attn_gain, 'shard', axis=0, tiled=True)]
    all_gather x1, blocking collectives: 12.5 us -> 108 us  [on_device(): lax.all_gather(mlp_gain, 'shard', axis=0, tiled=True)]
    all_gather x1, waiting for transfers between devices: 46.7 us -> 0.02 us  [on_device(): lax.all_gather(w_key, 'shard', axis=0, tiled=True)]
    all_gather x1, waiting for transfers between devices: 86.1 us -> 120 us  [on_device(): lax.all_gather(w_query, 'shard', axis=0, tiled=True)]
    unnamed x56 -> x91, local copies, waits for them, and re-layouts: 22.8 us -> 49.4 us
    all_gather x1, waiting for transfers between devices: 208 us -> 183 us  [on_device(): lax.all_gather(w_up, 'shard', axis=0, tiled=True)]
  transfers between devices with their start and end apart: 19 -> 22, of which waited for: 18 -> 16; matrix products, arithmetic and copies ran while one was open for 10% -> 11% of each run, Pallas kernels for 0% -> 0%
where the time goes in v1:
time: 2410 us
  waiting for transfers between devices  1840 us (76%)
  blocking collectives  249 us (10%)
  matrix products  203 us (8%)
  local copies, waits for them, and re-layouts  60.2 us (2%)
    psum x1, waiting for transfers between devices, on_device(): lax.psum((gains[0], owned_rows[0], owned_rows[1], owned_rows[2], owned_ro...  263 us
    all_gather x1, waiting for transfers between devices, on_device(): lax.all_gather(w_down, 'shard', axis=0, tiled=True)  208 us
    all_gather x1, waiting for transfers between devices, on_device(): lax.all_gather(w_gate, 'shard', axis=0, tiled=True)  193 us
    all_gather x1, waiting for transfers between devices, on_device(): lax.all_gather(w_up, 'shard', axis=0, tiled=True)  183 us
    all_gather x1, waiting for transfers between devices, on_device(): lax.all_gather(mlp_factors[2], 'shard', axis=0, tiled=True)  150 us
    all_gather x1, waiting for transfers between devices, on_device(): lax.all_gather(mlp_factors[3], 'shard', axis=0, tiled=True)  150 us
    all_gather x1, waiting for transfers between devices, on_device(): lax.all_gather(mlp_factors[1], 'shard', axis=0, tiled=True)  140 us
    all_gather x1, waiting for transfers between devices, on_device(): lax.all_gather(w_query, 'shard', axis=0, tiled=True)  120 us
  transfers between devices with their start and end apart: 22, of which 16 were waited for; matrix products, arithmetic and copies ran while one was open for 11% of the time, Pallas kernels for 0%

profile of v1, /device:TPU:0, one launch (start us, length us, event | category | flops | bytes accessed | tf_op | source)
XLA Modules:
  0.0 2405.7 jit_solution(18136732467212518752)
XLA Ops:
  13.0 5.1 collective-permute-start
  18.1 112.8 %all-gather = bf16[4,1,384]{2,1,0:T(2,128)(2,1)S(1)} all-gather(bf16[1,1,384]{2,1,0:T(2,128)(2,1)S(1)} %reshape.178), channel_id=1, replica_groups=mesh['replica'=8,'shard'=4] {'shard'}, dimensions={0}, use_global_device_ids=true | all-gather | bytes 3840 | tf_op jit(solution)/shard_map/all_gather | solution.py:253
  132.3 2.8 collective-permute-start.1
  135.8 2.3 fusion.63
  138.2 107.6 %all-gather.1 = bf16[4,1,384]{2,1,0:T(2,128)(2,1)S(1)} all-gather(bf16[1,1,384]{2,1,0:T(2,128)(2,1)S(1)} %reshape.180), channel_id=1, replica_groups=mesh['replica'=8,'shard'=4] {'shard'}, dimensions={0}, use_global_device_ids=true | all-gather | bytes 3840 | tf_op jit(solution)/shard_map/all_gather | solution.py:263
  246.8 1.8 constant_dynamic-update-slice_fusion.7
  248.6 4.1 constant_dynamic-update-slice_fusion.6
  252.7 3.4 convolution_convert_fusion.2
  257.4 3.0 fusion.94
  261.2 3.0 collective-permute-start.2
  264.2 4.0 constant_dynamic-update-slice_fusion.5
  268.2 120.0 %all-gather.25.cloned.1.call-done = bf16[1536,1536]{1,0:T(8,128)(2,1)} async-done(((bf16[384,1536]{1,0:T(8,128)(2,1)}), bf16[1536,1536]{1,0:T(8,128)(2,1)}) %all-gather.25.cloned.1.call-update) | async-done | bytes 4718608 | tf_op jit(solution)/shard_map/all_gather | solution.py:254
  388.2 4.5 fusion.95
  394.0 22.4 while.10
  416.4 68.5 %all-gather.27.cloned.1.call-done = bf16[1536,1536]{1,0:T(8,128)(2,1)} async-done(((bf16[384,1536]{1,0:T(8,128)(2,1)}), bf16[1536,1536]{1,0:T(8,128)(2,1)}) %all-gather.27.cloned.1.call-update) | async-done | bytes 4718608 | tf_op jit(solution)/shard_map/all_gather | solution.py:257
  484.9 4.3 multiply_reduce_fusion.3
  491.4 4.5 constant_dynamic-update-slice_fusion.4
  495.9 1.8 constant_dynamic-update-slice_fusion.3
  497.7 4.2 constant_dynamic-update-slice_fusion.2
  501.9 3.9 constant_dynamic-update-slice_fusion.1
  505.8 4.0 constant_dynamic-update-slice_fusion
  509.8 193.1 %all-gather.29.cloned.1.call-done = bf16[1536,4096]{1,0:T(8,128)(2,1)} async-done(((bf16[384,4096]{1,0:T(8,128)(2,1)}), bf16[1536,4096]{1,0:T(8,128)(2,1)}) %all-gather.29.cloned.1.call-update) | async-done | bytes 12582928 | tf_op jit(solution)/shard_map/all_gather | solution.py:264
  702.9 9.5 fusion.96
  712.5 208.3 %all-gather.31.cloned.1.call-done = bf16[4096,1536]{1,0:T(8,128)(2,1)} async-done(((bf16[1024,1536]{1,0:T(8,128)(2,1)}), bf16[4096,1536]{1,0:T(8,128)(2,1)}) %all-gather.31.cloned.1.call-update) | async-done | bytes 12582928 | tf_op jit(solution)/shard_map/all_gather | solution.py:266
  920.8 6.6 fusion.97
  927.4 18.0 multiply_convert_fusion
  945.5 10.0 fusion.98
  955.4 183.3 %all-gather.33.cloned.1.call-done = bf16[1536,4096]{1,0:T(8,128)(2,1)} async-done(((bf16[384,4096]{1,0:T(8,128)(2,1)}), bf16[1536,4096]{1,0:T(8,128)(2,1)}) %all-gather.33.cloned.1.call-update) | async-done | bytes 12582928 | tf_op jit(solution)/shard_map/all_gather | solution.py:274
  1138.7 9.4 multiply_reduce_fusion.1
  1150.7 3.7 convolution_convert_fusion.1
  1154.8 58.9 %while.27 = (s32[]{:T(128)}, f32[8,256,2,96]{1,3,2,0:T(8,128)}, f32[8,256,96]{1,2,0:T(8,128)}, bf16[8,256,96]{1,2,0:T(8,128)(2,1)}, bf16[8,256,96]{1,2,0:T(8,128...) while((s32[]{:T(128)}, f32[8,256,2,96]{1,3,2,0:T(8,128)}, ...), condition=%wide.region_9.10_spmd, body=%wide.region_7.9_spmd.sunk | while | flops 127731200 | bytes 6843497 | solution.py:149
  1159.5 1.8 fusion.168
  1166.9 1.8 fusion.168
  1174.2 1.8 fusion.168
  1181.6 1.8 fusion.168
  1196.3 1.8 fusion.168
  1222.4 29.6 %all-gather.39.cloned.1.call-done = bf16[1024,768]{0,1:T(8,128)(2,1)} async-done(((bf16[256,768]{0,1:T(8,128)(2,1)}), bf16[1024,768]{0,1:T(8,128)(2,1)}) %all-gather.39.cloned.1.call-update) | async-done | bytes 1572880 | tf_op jit(solution)/shard_map/all_gather | solution.py:309
  1252.0 3.5 fusion.78
  1255.5 33.9 %all-gather.41.cloned.1.call-done = bf16[1024,768]{0,1:T(8,128)(2,1)} async-done(((bf16[256,768]{0,1:T(8,128)(2,1)}), bf16[1024,768]{0,1:T(8,128)(2,1)}) %all-gather.41.cloned.1.call-update) | async-done | bytes 1572880 | tf_op jit(solution)/shard_map/all_gather | solution.py:310
  1289.3 3.5 fusion.76
  1292.8 59.7 %all-gather.37.cloned.1.call-done = bf16[1024,1536]{0,1:T(8,128)(2,1)} async-done(((bf16[256,1536]{0,1:T(8,128)(2,1)}), bf16[1024,1536]{0,1:T(8,128)(2,1)}) %all-gather.37.cloned.1.call-update) | async-done | bytes 3145744 | tf_op jit(solution)/shard_map/all_gather | solution.py:308
  1352.5 5.0 fusion.80
  1357.5 58.6 %all-gather.43.cloned.1.call-done = bf16[1024,1536]{0,1:T(8,128)(2,1)} async-done(((bf16[256,1536]{0,1:T(8,128)(2,1)}), bf16[1024,1536]{0,1:T(8,128)(2,1)}) %all-gather.43.cloned.1.call-update) | async-done | bytes 3145744 | tf_op jit(solution)/shard_map/all_gather | solution.py:311
  1416.2 63.2 %all-gather.45.cloned.1.call-done = bf16[1024,1536]{1,0:T(8,128)(2,1)} async-done(((bf16[256,1536]{1,0:T(8,128)(2,1)}), bf16[1024,1536]{1,0:T(8,128)(2,1)}) %all-gather.45.cloned.1.call-update) | async-done | bytes 3145744 | tf_op jit(solution)/shard_map/all_gather | solution.py:312
  1479.4 4.9 fusion.70
  1484.3 59.2 %all-gather.47.cloned.1.call-done = bf16[1024,1536]{1,0:T(8,128)(2,1)} async-done(((bf16[256,1536]{1,0:T(8,128)(2,1)}), bf16[1024,1536]{1,0:T(8,128)(2,1)}) %all-gather.47.cloned.1.call-update) | async-done | bytes 3145744 | tf_op jit(solution)/shard_map/all_gather | solution.py:281
  1543.5 150.3 %all-gather.51.cloned.1.call-done = bf16[1024,4096]{1,0:T(8,128)(2,1)} async-done(((bf16[256,4096]{1,0:T(8,128)(2,1)}), bf16[1024,4096]{1,0:T(8,128)(2,1)}) %all-gather.51.cloned.1.call-update) | async-done | bytes 8388624 | tf_op jit(solution)/shard_map/all_gather | solution.py:283
  1693.8 10.1 fusion.72
  1703.9 139.7 %all-gather.49.cloned.1.call-done = bf16[1024,4096]{1,0:T(8,128)(2,1)} async-done(((bf16[256,4096]{1,0:T(8,128)(2,1)}), bf16[1024,4096]{1,0:T(8,128)(2,1)}) %all-gather.49.cloned.1.call-update) | async-done | bytes 8388624 | tf_op jit(solution)/shard_map/all_gather | solution.py:282
  1843.6 9.8 fusion.74
  1853.4 53.2 %all-gather.55.cloned.1.call-done = bf16[1024,1536]{1,0:T(8,128)(2,1)} async-done(((bf16[256,1536]{1,0:T(8,128)(2,1)}), bf16[1024,1536]{1,0:T(8,128)(2,1)}) %all-gather.55.cloned.1.call-update) | async-done | bytes 3145744 | tf_op jit(solution)/shard_map/all_gather | solution.py:285
  1906.7 149.7 %all-gather.53.cloned.1.call-done = bf16[1024,4096]{1,0:T(8,128)(2,1)} async-done(((bf16[256,4096]{1,0:T(8,128)(2,1)}), bf16[1024,4096]{1,0:T(8,128)(2,1)}) %all-gather.53.cloned.1.call-update) | async-done | bytes 8388624 | tf_op jit(solution)/shard_map/all_gather | solution.py:284
  2056.4 8.9 fusion.59
  2067.2 4.5 fusion.99
  2073.7 2.4 fusion.69
  2076.0 15.7 all-reduce.4
  2091.9 13.3 all-reduce.2
  2105.2 3.7 fusion.66
  2108.9 7.7 fusion.58
  2116.6 262.9 %all-reduce.7.cloned.1.call-done = (f32[384,1536]{1,0:T(8,128)}, f32[384,768]{1,0:T(8,128)}, f32[384,768]{1,0:T(8,128)}, f32[384,1536]{1,0:T(8,128)}, f32[384,40...) async-done(((f32[384,1536]{1,0:T(8,128)}, f32[384,768]{1,0:T(8,128)}, f32[384,768]{1,0:T(8,128)}, f32[384,1536]{1,0:T(8,128)}, f32[384,4096]{1,0:T(8,128)}, ...) | async-done | bytes 25952272 | tf_op jit(solution)/shard_map/psum | solution.py:319
  2379.5 3.4 copy.98
  2388.3 3.2 copy.102
  2391.7 3.2 copy.103
  2396.3 2.7 copy.104
  (246 shorter events, 107.8 us)
Async XLA Ops:
  7.2 245.5 %all-gather.21.cloned.1.call-start = ((), (), s32[]{:S(2)}) async-start(), calls=%async_computation | async-start | bytes 2949120 | tf_op jit(solution)/shard_map/all_gather | solution.py:256
  7.9 249.4 %all-gather.23.cloned.1.call-start = ((), (), s32[]{:S(2)}) async-start(), calls=%async_computation.1 | async-start | bytes 2949120 | tf_op jit(solution)/shard_map/all_gather | solution.py:255
  8.7 379.6 %all-gather.25.cloned.1.call-start = ((), (), s32[]{:S(2)}) async-start(), calls=%async_computation.2 | async-start | bytes 5898240 | tf_op jit(solution)/shard_map/all_gather | solution.py:254
  9.4 475.5 %all-gather.27.cloned.1.call-start = ((), (), s32[]{:S(2)}) async-start(), calls=%async_computation.3 | async-start | bytes 5898240 | tf_op jit(solution)/shard_map/all_gather | solution.py:257
  10.0 693.0 %all-gather.29.cloned.1.call-start = ((), (), s32[]{:S(2)}) async-start(), calls=%async_computation.4 | async-start | bytes 15728640 | tf_op jit(solution)/shard_map/all_gather | solution.py:264
  10.6 910.2 %all-gather.31.cloned.1.call-start = ((), (), s32[]{:S(2)}) async-start(), calls=%async_computation.5 | async-start | bytes 15728640 | tf_op jit(solution)/shard_map/all_gather | solution.py:266
  10.6 7.5 copy-start.28
  11.1 1.9 copy-start
  11.1 1127.6 %all-gather.33.cloned.1.call-start = ((), (), s32[]{:S(2)}) async-start(), calls=%async_computation.6 | async-start | bytes 15728640 | tf_op jit(solution)/shard_map/all_gather | solution.py:274
  11.9 126.3 %copy-start.29 = (bf16[384]{0:T(512)(128)(2,1)S(1)}, bf16[384]{0:T(512)(128)(2,1)}, u32[]{:S(2)}) copy-start(bf16[384]{0:T(512)(128)(2,1)} %param.22) | copy-start | bytes 2308
  11.9 1210.5 %all-gather.35.cloned.1.call-start = ((), (), s32[]{:S(2)}) async-start(), calls=%async_computation.7 | async-start | bytes 3932160 | tf_op jit(solution)/shard_map/all_gather | solution.py:307
  13.0 119.3 %collective-permute-start = (bf16[384,4096]{1,0:T(8,128)(2,1)S(1)}, bf16[384,4096]{1,0:T(8,128)(2,1)}, u32[]{:S(2)}, u32[]{:S(2)}) collective-permute-start(bf16[384,4096]{1,0:T(8,128)(2,1)S(1)} %copy-done), channel_id=1, source_target_pairs={{0,3},{1,0},{2,1},{3,2},{4,7},{5,4},{6,5},{7,6},{8,11},{9,8},{10,9... | collective-permute-start | bytes 9437192 | tf_op jit(solution)/shard_map/ppermute | solution.py:16
  132.3 128.9 %collective-permute-start.1 = (bf16[384,4096]{1,0:T(8,128)(2,1)}, bf16[384,4096]{1,0:T(8,128)(2,1)}, u32[]{:S(2)}, u32[]{:S(2)}) collective-permute-start(bf16[384,4096]{1,0:T(8,128)(2,1)} %collective-permute-done), channel_id=1, source_target_pairs={{0,3},{1,0},{2,1},{3,2},{4,7},{5,4},{6,5},{7,6},{8,11},{9,8},{10,9... | collective-permute-start | bytes 9437192 | tf_op jit(solution)/shard_map/ppermute | solution.py:16
  135.7 2.4 copy-start.25
  138.0 1113.9 %all-gather.39.cloned.1.call-start = ((), (), s32[]{:S(2)}) async-start(), calls=%async_computation.9 | async-start | bytes 1966080 | tf_op jit(solution)/shard_map/all_gather | solution.py:309
  257.3 3.0 copy-start.17
  257.4 3.0 copy-start.20
  261.2 230.2 %collective-permute-start.2 = (bf16[384,4096]{1,0:T(8,128)(2,1)}, bf16[384,4096]{1,0:T(8,128)(2,1)}, u32[]{:S(2)}, u32[]{:S(2)}) collective-permute-start(bf16[384,4096]{1,0:T(8,128)(2,1)} %collective-permute-done.1), channel_id=1, source_target_pairs={{0,3},{1,0},{2,1},{3,2},{4,7},{5,4},{6,5},{7,6},{8,11},{9,8},{10,9... | collective-permute-start | bytes 9437192 | tf_op jit(solution)/shard_map/ppermute | solution.py:16
  388.2 4.5 copy-start.18
  388.2 4.6 copy-start.21
  416.4 72.8 %copy-start.14 = (bf16[8,256,96]{1,2,0:T(8,128)(2,1)}, bf16[8,256,96]{1,2,0:T(8,128)(2,1)S(1)}, u32[]{:S(2)}) copy-start(bf16[8,256,96]{1,2,0:T(8,128)(2,1)S(1)} %get-tuple-element.460) | copy-start | bytes 1179652
  489.2 1.1 copy-start.2
  505.8 197.1 %copy-start.9 = (bf16[256,1536]{1,0:T(8,128)(2,1)S(1)}, bf16[256,1536]{1,0:T(8,128)(2,1)}, u32[]{:S(2)}) copy-start(bf16[256,1536]{1,0:T(8,128)(2,1)} %multiply_convert_fusion.3) | copy-start | bytes 2359300
  509.8 410.9 %copy-start.6 = (bf16[256,1536]{1,0:T(8,128)(2,1)S(1)}, bf16[256,1536]{1,0:T(8,128)(2,1)}, u32[]{:S(2)}) copy-start(bf16[256,1536]{1,0:T(8,128)(2,1)} %param.16) | copy-start | bytes 2359300
  920.8 6.6 copy-start.31
  945.4 193.3 %copy-start.3 = (f32[256,1536]{1,0:T(8,128)S(1)}, f32[256,1536]{1,0:T(8,128)}, u32[]{:S(2)}) copy-start(f32[256,1536]{1,0:T(8,128)} %copy-done.2) | copy-start | bytes 4718596
  1149.8 0.9 copy-start.7
  1154.7 58.9 %copy-start.19 = (f32[256,48]{0,1:T(8,128)S(1)}, f32[256,48]{0,1:T(8,128)}, u32[]{:S(2)}) copy-start(f32[256,48]{0,1:T(8,128)} %get-tuple-element.215) | copy-start | bytes 147460
  1154.7 58.9 %copy-start.22 = (f32[256,48]{0,1:T(8,128)S(1)}, f32[256,48]{0,1:T(8,128)}, u32[]{:S(2)}) copy-start(f32[256,48]{0,1:T(8,128)} %get-tuple-element.216) | copy-start | bytes 147460
  1213.6 2.8 copy-start.15
  1215.8 73.5 %all-gather.41.cloned.1.call-start = ((), (), s32[]{:S(2)}) async-start(), calls=%async_computation.10 | async-start | bytes 1966080 | tf_op jit(solution)/shard_map/all_gather | solution.py:310
  1216.4 136.1 %all-gather.37.cloned.1.call-start = ((), (), s32[]{:S(2)}) async-start(), calls=%async_computation.8 | async-start | bytes 3932160 | tf_op jit(solution)/shard_map/all_gather | solution.py:308
  1217.7 198.5 %all-gather.43.cloned.1.call-start = ((), (), s32[]{:S(2)}) async-start(), calls=%async_computation.11 | async-start | bytes 3932160 | tf_op jit(solution)/shard_map/all_gather | solution.py:311
  1218.2 261.1 %all-gather.45.cloned.1.call-start = ((), (), s32[]{:S(2)}) async-start(), calls=%async_computation.12 | async-start | bytes 3932160 | tf_op jit(solution)/shard_map/all_gather | solution.py:312
  1219.0 324.5 %all-gather.47.cloned.1.call-start = ((), (), s32[]{:S(2)}) async-start(), calls=%async_computation.13 | async-start | bytes 3932160 | tf_op jit(solution)/shard_map/all_gather | solution.py:281
  1219.6 474.2 %all-gather.51.cloned.1.call-start = ((), (), s32[]{:S(2)}) async-start(), calls=%async_computation.15 | async-start | bytes 10485760 | tf_op jit(solution)/shard_map/all_gather | solution.py:283
  1220.1 623.5 %all-gather.49.cloned.1.call-start = ((), (), s32[]{:S(2)}) async-start(), calls=%async_computation.14 | async-start | bytes 10485760 | tf_op jit(solution)/shard_map/all_gather | solution.py:282
  1220.7 686.0 %all-gather.55.cloned.1.call-start = ((), (), s32[]{:S(2)}) async-start(), calls=%async_computation.17 | async-start | bytes 3932160 | tf_op jit(solution)/shard_map/all_gather | solution.py:285
  1221.3 835.1 %all-gather.53.cloned.1.call-start = ((), (), s32[]{:S(2)}) async-start(), calls=%async_computation.16 | async-start | bytes 10485760 | tf_op jit(solution)/shard_map/all_gather | solution.py:284
  1221.9 1157.7 %all-reduce.7.cloned.1.call-start = ((), (), s32[]{:S(2)}) async-start(), calls=%async_computation.18 | async-start | bytes 51904512 | tf_op jit(solution)/shard_map/psum | solution.py:319
  2065.3 0.7 copy-start.30
  2065.3 1.9 copy-start.8
  2067.2 4.5 copy-start.5
  2067.2 4.5 copy-start.12
  2071.7 1.1 copy-start.1
  2071.7 1.9 copy-start.10
  2071.8 1.9 copy-start.16
  2071.8 1.9 copy-start.26
  2073.7 31.5 %copy-start.27 = (f32[256]{0:T(256)S(1)}, f32[256]{0:T(256)}, u32[]{:S(2)}) copy-start(f32[256]{0:T(256)} %get-tuple-element.211) | copy-start | bytes 3076
  2105.2 3.7 copy-start.13
  2379.5 3.4 copy-start.24
  2379.5 4.4 copy-start.23
  2382.9 2.3 copy-start.11
  2383.9 4.3 copy-start.4
  2385.2 6.2 slice-start.2
  2388.3 3.4 slice-start.3
  2388.3 7.0 slice-start
  2391.7 4.6 slice-start.1
Sparse Core Ops, SparseCore 0:
  9.6 87.0 all-gather.20
  98.2 110.7 all-gather.22
  210.5 177.6 all-gather.24
  389.6 95.2 all-gather.26
  486.3 216.5 all-gather.28
  704.4 216.3 all-gather.30
  922.3 216.3 all-gather.32
  1140.9 61.6 all-gather.34
  1215.9 35.9 all-gather.38
  1253.4 35.9 all-gather.40
  1290.9 61.6 all-gather.36
  1354.5 61.5 all-gather.42
  1417.7 61.6 all-gather.44
  1481.4 62.0 all-gather.46
  1545.5 148.2 all-gather.50
  1695.8 147.7 all-gather.48
  1845.0 61.6 all-gather.54
  1908.1 148.2 all-gather.52
  2065.4 314.0 all-reduce.6
